TPU v7x, 32 devices: a whole 2x2x4 slice. The times are simulated.
32 devices in a mesh: seq: 4 (over y, x), fsdp: 8 (over z, core).
Axes of the slice: x: 2, y: 2, z: 4, core: 2. Of those that a mesh axis runs over, the one named last changes fastest.
Arguments:
- tokens: bfloat16 [16, 1536, 1536], P('fsdp', 'seq'), may hold values from -6 to 6
- lengths: int32 [16], P('fsdp'), may hold values from 384 to 1536, as said below
- norm_gain: bfloat16 [1536], P('fsdp'), may hold values from 0.099609375 to 1.8984375
- in_weight: bfloat16 [1536, 4608], P('fsdp'), may hold values from -0.15625 to 0.15625
- conv_weight: bfloat16 [3, 1536], P(None, 'fsdp'), may hold values from -3 to 3
- out_weight: bfloat16 [1536, 1536], P('fsdp'), may hold values from -0.15625 to 0.15625
- ffn_gain: bfloat16 [1536], P('fsdp'), may hold values from 0.099609375 to 1.8984375
- gate_weight: bfloat16 [1536, 6912], P('fsdp'), may hold values from -0.15625 to 0.15625
- up_weight: bfloat16 [1536, 6912], P('fsdp'), may hold values from -0.15625 to 0.15625
- down_weight: bfloat16 [6912, 1536], P('fsdp'), may hold values from -0.078125 to 0.078125
- cotangent: bfloat16 [16, 1536, 1536], P('fsdp', 'seq'), may hold values from -6 to 6
Outputs:
- output: bfloat16 [16, 1536, 1536], P('fsdp', 'seq')
- tokens_grad: float32 [16, 1536, 1536], P('fsdp', 'seq')
- norm_gain_grad: float32 [1536], P('fsdp')
- in_weight_grad: float32 [1536, 4608], P('fsdp')
- conv_weight_grad: float32 [3, 1536], P(None, 'fsdp')
- out_weight_grad: float32 [1536, 1536], P('fsdp')
- ffn_gain_grad: float32 [1536], P('fsdp')
- gate_weight_grad: float32 [1536, 6912], P('fsdp')
- up_weight_grad: float32 [1536, 6912], P('fsdp')
- down_weight_grad: float32 [6912, 1536], P('fsdp')
Inputs may be any that keep to these rules, and one draw needn't show every extreme that they name: `lengths`: each sequence's valid positions come first; at least one sequence is full length.
All inputs are finite; a program needn't handle non-finite values.
Results may differ from a plain program's by a relative error of at most 0.018.
Values may be sent and summed in bfloat16 or wider, within the bound.
A program may use at most 384 MiB of HBM per device.

v0:
```python
import functools

import jax
import jax.numpy as jnp
from jax import lax
from jax.experimental import pallas as pl
from jax.experimental.pallas import tpu as pltpu
from jax.sharding import PartitionSpec as P

EPS = 1e-05
MESH = pl.DeviceIdType.MESH

DMA = pltpu.SemaphoreType.DMA
ANY = pl.BlockSpec(memory_space=pl.ANY)


def rem(t, n):
    return t % n if isinstance(t, int) else lax.rem(t, n)


def remote(src, dst, send, recv, to):
    return pltpu.make_async_remote_copy(src_ref=src, dst_ref=dst, send_sem=send, recv_sem=recv, device_id=to, device_id_type=MESH)


class Here:
    def __init__(self):
        s, f = lax.axis_index("seq"), lax.axis_index("fsdp")
        self.s, self.f = s, f
        self.z, self.c = f // 2, lax.rem(f, 2)
        self.s0, self.s1 = lax.rem(s, 2), s // 2
        self.mate = (s, f + 1 - 2 * self.c)
        self.beside = (s + 1 - 2 * self.s0, s + 2 - 4 * self.s1)

    def greet(self, along=False):
        barrier = pltpu.get_barrier_semaphore()
        peers = [self.mate] + [(b, self.f) for b in self.beside] + [(self.s, lax.rem(self.f + 2 * j, 8)) for j in (1, 2, 3)]
        for peer in peers:
            pl.semaphore_signal(barrier, inc=1, device_id=peer, device_id_type=MESH)
        count = len(peers)
        if along:
            before, after = self.s > 0, self.s < 3
            for there, step in ((before, -1), (after, 1)):

                @pl.when(there)
                def _(step=step):
                    pl.semaphore_signal(barrier, inc=1, device_id=(jnp.clip(self.s + step, 0, 3), self.f), device_id_type=MESH)

            count = count + jnp.where(before, 1, 0) + jnp.where(after, 1, 0)
        pl.semaphore_wait(barrier, count)


class Reducer:
    def __init__(self, here, paired, held, total, fresh, landing, sems, core_source, goal):
        self.here, self.paired = here, paired
        self.held, self.fresh, self.total, self.landing = held, fresh, total, landing
        (self.local, self.core_s, self.core_r, self.one_s, self.one_r, self.two_s, self.two_r) = sems[:7]
        (self.z_s, self.z_r, self.near_s, self.near_r, self.far_s, self.far_r) = sems[7:]
        self.core_source, self.goal = core_source, goal
        self.slots, self.chips = held.shape[0], held.shape[2]

    def mine(self, t):
        return self.held.at[rem(t, self.slots)]

    def to_core(self, t):
        return remote(self.core_source(t), self.landing[0].at[t], self.core_s.at[t], self.core_r.at[t], self.here.mate)

    def one(self, t, d):
        h = self.here
        src = self.mine(t).at[0, :, :, 1 - h.s0] if d == 0 else self.mine(t).at[1, :, 1 - h.s1]
        return remote(src, self.landing[1 + d].at[t], self.one_s.at[t, d], self.one_r.at[t, d], (h.beside[d], h.f))

    def two(self, t, d):
        h = self.here
        src = self.mine(t).at[1, :, h.s1, 1 - h.s0] if d == 0 else self.mine(t).at[0, :, 1 - h.s1, h.s0]
        return remote(src, self.landing[4 - d].at[t], self.two_s.at[t, d], self.two_r.at[t, d], (h.beside[d], h.f))

    def part(self, t, a):
        h = self.here
        if self.paired:
            return self.mine(t).at[:, a, h.s1, h.s0]
        return self.mine(t).at[a // 2, lax.rem(a, 2), h.s1, h.s0]

    def to_chip(self, t, j):
        h = self.here
        a = lax.rem(h.z + j, 4)
        slot = jnp.where(h.z < a, h.z, h.z - 1)
        return remote(self.part(t, a), self.landing[5].at[t, slot], self.z_s.at[t, j - 1], self.z_r.at[t, slot], (h.s, 2 * a + h.c))

    def from_chip(self, t, slot):
        h = self.here
        return remote(self.part(t, 0), self.landing[5].at[t, slot], self.z_s.at[t, 0], self.z_r.at[t, slot], h.mate)

    def keep(self, t):
        return pltpu.make_async_copy(self.total.at[rem(t, 2)], self.goal(t, self.here.s, None), self.local.at[8 + rem(t, 2)])

    def near(self, t, d):
        h = self.here
        return remote(self.total.at[rem(t, 2)], self.goal(t, h.s, None), self.near_s.at[t, d], self.near_r.at[t, d], (h.beside[d], h.f))

    def far(self, t, d):
        h = self.here
        ref = self.goal(t, h.beside[1 - d], d)
        return remote(ref, ref, self.far_s.at[t, d], self.far_r.at[t, d], (h.beside[d], h.f))

    def pending(self, src, dst, which):
        return pltpu.make_async_copy(src, dst, self.local.at[which])

    def bring(self, src, dst, which):
        self.pending(src, dst, which).start()

    def stage0(self, t):
        self.to_core(t).start()

    def fetch1(self, t):
        self.to_core(t).wait_recv()
        self.bring(self.landing[0].at[t], self.fresh[0], 0)

    def stage1(self, t):
        fresh, me = self.fresh[0], self.mine(t)
        self.pending(self.landing[0].at[t], fresh, 0).wait()

        @pl.loop(0, 2 * self.chips)
        def _(i):
            at = (i // self.chips, lax.rem(i, self.chips))
            me[at] = me[at] + fresh[at]

        self.one(t, 0).start()
        self.one(t, 1).start()

    def fetch2(self, t):
        for d in (0, 1):
            self.one(t, d).wait_recv()
            self.bring(self.landing[1 + d].at[t], self.fresh[1].at[d], 1 + d)

    def stage2(self, t):
        h, fresh, me = self.here, self.fresh[1], self.mine(t)
        for d in (0, 1):
            self.pending(self.landing[1 + d].at[t], fresh.at[d], 1 + d).wait()

        @pl.loop(0, self.chips)
        def _(a):
            for b in (0, 1):
                me[0, a, b, h.s0] = me[0, a, b, h.s0] + fresh[0, a, b]
                me[1, a, h.s1, b] = me[1, a, h.s1, b] + fresh[1, a, b]

        self.two(t, 1).start()
        self.two(t, 0).start()

    def fetch3(self, t):
        for d in (1, 0):
            self.two(t, d).wait_recv()
            self.bring(self.landing[4 - d].at[t], self.fresh[2].at[1 - d], 4 - d)

    def stage3(self, t):
        h, fresh, me = self.here, self.fresh[2], self.mine(t)
        for d in (1, 0):
            self.pending(self.landing[4 - d].at[t], fresh.at[1 - d], 4 - d).wait()

        @pl.loop(0, self.chips)
        def _(a):
            me[0, a, h.s1, h.s0] = me[0, a, h.s1, h.s0] + fresh[0, a]
            me[1, a, h.s1, h.s0] = me[1, a, h.s1, h.s0] + fresh[1, a]

        for j in (1, 2, 3):
            self.to_chip(t, j).start()

    def fetch4(self, t):
        for slot in range(3):
            self.from_chip(t, slot).wait_recv()
            self.bring(self.landing[5].at[t, slot], self.fresh[3].at[slot], 5 + slot)

    def stage4(self, t):
        h, fresh = self.here, self.fresh[3]
        for slot in range(3):
            self.pending(self.landing[5].at[t, slot], fresh.at[slot], 5 + slot).wait()
        acc = self.part(t, h.z)[...].astype(jnp.float32)
        for slot in range(3):
            acc += fresh[slot].astype(jnp.float32)
        self.total[rem(t, 2)] = acc.astype(jnp.bfloat16)
        self.near(t, 0).start()
        self.near(t, 1).start()
        self.keep(t).start()
        for d in (0, 1):
            self.one(t, d).wait_send()
            self.two(t, d).wait_send()
        for j in (1, 2, 3):
            self.to_chip(t, j).wait_send()

    def near_in(self, t, d):
        h = self.here
        ref = self.goal(t, h.beside[d], None)
        return remote(ref, ref, self.near_s.at[t, d], self.near_r.at[t, d], (h.beside[d], h.f))

    def far_in(self, t, d):
        h = self.here
        ref = self.goal(t, 3 - h.s, d)
        return remote(ref, ref, self.far_s.at[t, d], self.far_r.at[t, d], (h.beside[d], h.f))

    def stage5(self, t):
        self.near_in(t, 1).wait_recv()
        self.far(t, 0).start()
        self.near_in(t, 0).wait_recv()
        self.far(t, 1).start()
        self.near(t, 0).wait_send()
        self.near(t, 1).wait_send()
        self.keep(t).wait()

    def stage6(self, t):
        for d in (0, 1):
            self.far_in(t, d).wait_recv()
            self.far(t, d).wait_send()


def landing_shapes(n, paired, rows, width):
    chips = 4 if paired else 2
    lead = (2,) if paired else ()
    shapes = [(n, 2, chips, 2, 2, rows, width)] + [(n, chips, 2, rows, width)] * 2 + [(n, chips, rows, width)] * 2 + [(n, 3) + lead + (rows, width)]
    return [jax.ShapeDtypeStruct(shape, jnp.bfloat16) for shape in shapes]


def scratch_shapes(slots, paired, rows, width):
    chips = 4 if paired else 2
    lead = (2,) if paired else ()
    shapes = [(slots, 2, chips, 2, 2, rows, width), (2,) + lead + (rows, width)]
    shapes += [(2, chips, 2, 2, rows, width), (2, chips, 2, rows, width), (2, chips, rows, width), (3,) + lead + (rows, width)]
    return [pltpu.VMEM(shape, jnp.bfloat16) for shape in shapes]


def sem_shapes(n):
    return [DMA((10,)), DMA((n,)), DMA((n,))] + [DMA((n, 2))] * 4 + [DMA((n, 3))] * 2 + [DMA((n, 2))] * 4


def halves(rows):
    half = (rows // 2 + 7) // 8 * 8
    return {None: pl.ds(0, rows), 0: pl.ds(0, half), 1: pl.ds(half, rows - half)}


TILE = 256
SUBS = 3
SLOTS = 5


def dot_nn(a, b):
    return lax.dot_general(a, b, (((1,), (0,)), ((), ())), preferred_element_type=jnp.float32)


def dot_nt(a, b):
    return lax.dot_general(a, b, (((1,), (1,)), ((), ())), preferred_element_type=jnp.float32)


def dot_tn(a, b):
    return lax.dot_general(a, b, (((0,), (0,)), ((), ())), preferred_element_type=jnp.float32)


def ffn_kernel(tiles, n2, mine_t, mate_t, down_in, keep, w_gate, w_up, w_down, hidden, *refs):
    output, back, grad_down, shards = refs[:4]
    landing = refs[4:10]
    act, gate_back, up_back, outgoing, held, total = refs[10:16]
    fresh, sems = refs[16:20], refs[20:33]
    y, start_sem = refs[33:]
    hidden_in = pltpu.make_async_copy(hidden, y, start_sem)
    i = pl.program_id(0)
    chunks = tiles // SUBS
    here = Here()
    width = TILE * SUBS
    rows = shards.shape[2]
    spans = halves(rows)

    def goal(t, quarter, part):
        return shards.at[:, quarter, spans[part], pl.ds(pl.multiple_of(t * width, width), width)]

    red = Reducer(here, True, held, total, fresh, landing, sems, lambda t: outgoing.at[lax.rem(t, 2)], goal)

    def hook(offset, *stages):
        past = i - offset
        t = past // SUBS

        @pl.when((past >= 0) & (lax.rem(past, SUBS) == 0) & (t < chunks))
        def _():
            for stage in stages:
                stage(t)

    @pl.when(i == 0)
    def _():
        here.greet()
        hidden_in.start()
        back[...] = jnp.zeros_like(back)

    @pl.when(i < tiles)
    def _():
        g = dot_nn(n2[...], w_gate[...])
        u = dot_nn(n2[...], w_up[...])
        a = dot_nt(down_in[...], w_down[...])
        sig = jax.nn.sigmoid(g)
        silu = g * sig
        act[...] = (silu * u).astype(jnp.bfloat16)
        gate_back[...] = (a * u * (sig * (1.0 + g * (1.0 - sig)))).astype(jnp.bfloat16)
        up_back[...] = (a * silu).astype(jnp.bfloat16)

    hook(7, red.stage2)
    hook(13, red.fetch4)

    @pl.when(i == 0)
    def _():
        hidden_in.wait()

    @pl.when(i == tiles)
    def _():
        output[...] = (y[...] * keep[...]).astype(jnp.bfloat16)

    @pl.when(i < tiles)
    def _():
        @pl.loop(0, 3)
        def _(j):
            at = pl.ds(pl.multiple_of(j * 512, 512), 512)
            y[:, at] += dot_nn(act[...], w_down[:, at])
            back[:, at] += dot_nt(gate_back[...], w_gate[at, :]) + dot_nt(up_back[...], w_up[at, :])
            grad_down[:, at] = dot_tn(act[...], down_in[:, at]).astype(jnp.bfloat16)

    hook(3, red.fetch1)
    hook(10, red.fetch3)
    chunk, sub = i // SUBS, lax.rem(i, SUBS)

    @pl.when((sub == 0) & (chunk >= 2) & (chunk < chunks + 2))
    def _():
        red.to_core(chunk - 2).wait_send()

    @pl.when(i < tiles)
    def _():
        at = pl.ds(pl.multiple_of(sub * TILE, TILE), TILE)
        out, me = outgoing.at[lax.rem(chunk, 2)], red.mine(chunk)
        shape = (4, 2, 2, rows, TILE)
        for m, grad in ((0, gate_back), (1, up_back)):
            out[m, :, :, :, :, at] = dot_nn(mate_t[...], grad[...]).astype(jnp.bfloat16).reshape(shape)
            me[m, :, :, :, :, at] = dot_nn(mine_t[...], grad[...]).astype(jnp.bfloat16).reshape(shape)

    hook(3, red.stage1)
    hook(6, red.fetch2)
    hook(10, red.stage3)
    hook(13, red.stage4)
    hook(16, red.stage5)
    hook(19, red.stage6)

    @pl.when((sub == SUBS - 1) & (chunk < chunks))
    def _():
        red.stage0(chunk)


def ffn(n2, mine_t, mate_t, down_in, keep, w_gate, w_up, w_down, hidden_one, cid):
    m, d = n2.shape
    hidden = w_gate.shape[1]
    tiles = hidden // TILE
    chunks, width = tiles // SUBS, TILE * SUBS
    rows = d // 32
    one = lambda *shape: pl.BlockSpec(shape, lambda i: (0, 0), pipeline_mode=pl.Buffered(1))
    across = pl.BlockSpec((d, TILE), lambda i: (0, jnp.minimum(i, tiles - 1)))
    down = pl.BlockSpec((TILE, d), lambda i: (jnp.minimum(i, tiles - 1), 0))
    out_shape = [jax.ShapeDtypeStruct((m, d), jnp.bfloat16), jax.ShapeDtypeStruct((m, d), jnp.float32)] + [jax.ShapeDtypeStruct((hidden, d), jnp.bfloat16), jax.ShapeDtypeStruct((2, 4, rows, hidden), jnp.bfloat16)]
    out_shape += landing_shapes(chunks, True, rows, width)
    res = pl.pallas_call(
        functools.partial(ffn_kernel, tiles),
        grid=(tiles + 17,),
        out_shape=out_shape,
        in_specs=[one(m, d), one(d // 2, m), one(d // 2, m), one(m, d), one(m, 1), across, across, down, ANY],
        out_specs=[one(m, d), one(m, d), down, ANY] + [ANY] * 6,
        scratch_shapes=[pltpu.VMEM((m, TILE), jnp.bfloat16)] * 3
        + [pltpu.VMEM((2, 2, 4, 2, 2, rows, width), jnp.bfloat16)]
        + scratch_shapes(SLOTS, True, rows, width)
        + sem_shapes(chunks)
        + [pltpu.VMEM((m, d), jnp.float32), DMA],
        compiler_params=pltpu.CompilerParams(collective_id=cid, has_side_effects=True, vmem_limit_bytes=61 << 20),
        name="ffn",
    )(n2, mine_t, mate_t, down_in, keep, w_gate, w_up, w_down, hidden_one)
    return res[:4]


def front_kernel(count, *refs):
    shards, small, tokens = refs[:count], refs[count], refs[count + 1]
    at = count + 2
    fulls = refs[at : at + count]
    normed_one, projected, edges, vectors, hidden_out, normed_two, mine_t, mate_t = refs[at + count : at + count + 8]
    at += count + 8
    (local_sem, core_send, core_recv, z_send, z_recv, near_send, near_recv, far_send, far_recv, small_send, small_recv) = refs[at : at + 11]
    at += 11
    staged = refs[at : at + count]
    smalls, weights, part, mixed, gated, hidden, turned, work_sem, edge_s, edge_r = refs[at + count :]
    s, f = lax.axis_index("seq"), lax.axis_index("fsdp")
    z, c = f // 2, lax.rem(f, 2)
    mate = f + 1 - 2 * c
    beside = (s + 1 - 2 * lax.rem(s, 2), s + 2 - 4 * (s // 2))
    last = 3
    flip = z >= 2
    zf = jnp.where(flip, last - z, z)

    def source(j):
        a = jnp.where(j < zf, j, j + 1)
        return jnp.where(flip, last - a, a)

    def slot(at, a):
        turned = at >= 2
        at = jnp.where(turned, last - at, at)
        a = jnp.where(turned, last - a, a)
        return jnp.where(a < at, a, a - 1)

    barrier = pltpu.get_barrier_semaphore()
    for k in range(1, 8):
        pl.semaphore_signal(barrier, inc=1, device_id=(s, lax.rem(f + k, 8)), device_id_type=MESH)
    for b in beside:
        pl.semaphore_signal(barrier, inc=1, device_id=(b, f), device_id_type=MESH)
    before, after = s > 0, s < 3
    for there, step in ((before, -1), (after, 1)):

        @pl.when(there)
        def _(step=step):
            pl.semaphore_signal(barrier, inc=1, device_id=(jnp.clip(s + step, 0, 3), f), device_id_type=MESH)

    pl.semaphore_wait(barrier, 9 + jnp.where(before, 1, 0) + jnp.where(after, 1, 0))

    def remote(src, dst, send, recv, to):
        return pltpu.make_async_remote_copy(src_ref=src, dst_ref=dst, send_sem=send, recv_sem=recv, device_id=to, device_id_type=MESH)

    def rows(m, shard_index, quarter=None, part=None):
        r = shards[m].shape[0]
        start, size = shard_index * r, r
        if quarter is not None:
            size = r // 4
            start = start + quarter * size
            half = (size // 2 + 7) // 8 * 8
            if part == 0:
                size = half
            elif part == 1:
                start, size = start + half, size - half
        return pl.ds(pl.multiple_of(start, 8), size)

    def place(m, *where):
        return fulls[m].at[rows(m, *where)]

    def load(m):
        return pltpu.make_async_copy(shards[m], staged[m], local_sem.at[m])

    def keep(m):
        return pltpu.make_async_copy(staged[m], place(m, f), local_sem.at[m])

    def own_core(m):
        return remote(shards[m], place(m, f), core_send.at[m, 3], core_recv.at[m, 3], (s, mate))

    def z_own(m, up):
        to = z + 1 if up else z - 1
        return remote(shards[m].at[rows(m, 0, s)], place(m, f, s), z_send.at[m, 3 + up], z_recv.at[m, slot(to, z)], (s, 2 * to + c))

    def z_on(m, j):
        a = source(j)
        to = jnp.where(a < z, z + 1, z - 1)
        at = place(m, 2 * a + c, s)
        to_safe = jnp.clip(to, 0, last)
        return remote(at, at, z_send.at[m, j], z_recv.at[m, jnp.clip(slot(to_safe, a), 0, 2)], (s, 2 * to_safe + c))

    def z_in(m, j):
        at = place(m, 2 * source(j) + c, s)
        return remote(at, at, z_send.at[m, j], z_recv.at[m, j], (s, f))

    def goes_on(j):
        a = source(j)
        return jnp.where(a < z, z < last, z > 0)

    def near(m, j, d):
        at = place(m, 2 * source(j) + c, s)
        return remote(at, at, near_send.at[m, j, d], near_recv.at[m, j, d], (beside[d], f))

    def far(m, j, d):
        at = place(m, 2 * source(j) + c, beside[1 - d], d)
        return remote(at, at, far_send.at[m, j, d], far_recv.at[m, j, d], (beside[d], f))

    def core(m, j):
        at = place(m, 2 * source(j) + c)
        return remote(at, at, core_send.at[m, j], core_recv.at[m, j], (s, mate))

    def begin(m):
        @pl.when(z < last)
        def _():
            z_own(m, 1).start()
        @pl.when(z > 0)
        def _():
            z_own(m, 0).start()
        load(m).start()
        own_core(m).start()

    def spread(m, j):
        z_in(m, j).wait_recv()
        @pl.when(goes_on(j))
        def _():
            z_on(m, j).start()
        near(m, j, 0).start()
        near(m, j, 1).start()
        if j == 0:
            load(m).wait()
            keep(m).start()

    def diagonal(m, j):
        near(m, j, 1).wait_recv()
        far(m, j, 0).start()
        near(m, j, 0).wait_recv()
        far(m, j, 1).start()

    def share(m, j):
        far(m, j, 0).wait_recv()
        far(m, j, 1).wait_recv()
        core(m, j).start()

    def finish(m, j):
        if j == 0:
            keep(m).wait()
            own_core(m).wait()
            @pl.when(z < last)
            def _():
                z_own(m, 1).wait_send()
            @pl.when(z > 0)
            def _():
                z_own(m, 0).wait_send()
        @pl.when(goes_on(j))
        def _():
            z_on(m, j).wait_send()
        for d in (0, 1):
            near(m, j, d).wait_send()
            far(m, j, d).wait_send()
        core(m, j).wait()

    def small_copy(k):
        return remote(small, smalls.at[f], small_send.at[k - 1], small_recv.at[k - 1], (s, lax.rem(f + k, 8)))

    depth = tokens.shape[1]
    blocks = depth // 256
    seqs, length = mixed.shape[0], mixed.shape[1] - 8
    gain_one, taps, gain_two = 0, 1, 4

    def small_step():
        vectors[...] = jnp.zeros(vectors.shape, jnp.float32)
        for k in range(8):
            if k:
                small_copy(k).wait()
            start = lax.rem(f + 8 - k, 8) * (depth // 8) // 128 * 128
            at = pl.ds(pl.multiple_of(start, 128), small.shape[1])
            vectors[:, at] = vectors[:, at] + (smalls[k - 1] if k else small[...])

    def norm_one_step():
        @pl.loop(0, tokens.shape[0] // 64)
        def _(r):
            at = pl.ds(pl.multiple_of(r * 64, 64), 64)
            token_rows = tokens[at, :].astype(jnp.float32)
            scale = lax.rsqrt(jnp.mean(token_rows * token_rows, -1, keepdims=True) + EPS)
            normed_one[at, :] = (token_rows * scale * vectors[gain_one : gain_one + 1, :]).astype(jnp.bfloat16)

    def weight_in(j):
        slot = j % 2
        return [
            pltpu.make_async_copy(fulls[1].at[:, pl.ds(g * depth + j * 256, 256)], weights.at[slot, g], work_sem.at[3 * slot + g])
            for g in range(3)
        ]

    def part_out(j):
        slot = j % 2
        return [
            pltpu.make_async_copy(part.at[slot, g], projected.at[:, pl.ds(g * depth + j * 256, 256)], work_sem.at[6 + 3 * slot + g])
            for g in range(3)
        ]

    def start_all(copies):
        for copy in copies:
            copy.start()

    def wait_all(copies):
        for copy in copies:
            copy.wait()

    def project_step(j):
        slot, at = j % 2, slice(j * 256, (j + 1) * 256)
        if j == 0:
            start_all(weight_in(0))
        wait_all(weight_in(j))
        if j + 1 < blocks:
            start_all(weight_in(j + 1))
        if j >= 2:
            wait_all(part_out(j - 2))
        for g in range(3):
            part[slot, g] = dot_nn(normed_one[...], weights[slot, g]).astype(jnp.bfloat16)
        start_all(part_out(j))
        gated[:, at] = part[slot, 1]
        for q in range(seqs):
            span = slice(q * length, (q + 1) * length)
            mixed[q, 8:, at] = part[slot, 0, span, :].astype(jnp.float32) * part[slot, 2, span, :].astype(jnp.float32)

    def edge_copy():
        return remote(mixed.at[:, length : length + 8], mixed.at[:, 0:8], edge_s, edge_r, (jnp.minimum(s + 1, 3), f))

    def edge_start():
        wait_all(part_out(blocks - 2))
        wait_all(part_out(blocks - 1))

        @pl.when(jnp.logical_not(before))
        def _():
            mixed[:, 0:8, :] = jnp.zeros((seqs, 8, depth), jnp.float32)

        @pl.when(after)
        def _():
            edge_copy().start()

        start_all([out_in(0)])

    def edge_wait():
        @pl.when(after)
        def _():
            edge_copy().wait_send()

        @pl.when(before)
        def _():
            edge_copy().wait_recv()

        edges[...] = mixed[:, 0:8, :]

    def conv_step(j):
        at = slice(j * 256, (j + 1) * 256)
        for q in range(seqs):
            span = slice(q * length, (q + 1) * length)
            conv = sum(vectors[taps + k : taps + k + 1, at] * mixed[q, 6 + k : 6 + k + length, at] for k in range(3))
            gated[span, at] = (gated[span, at].astype(jnp.float32) * conv).astype(jnp.bfloat16)

    def out_in(j):
        return pltpu.make_async_copy(fulls[0].at[:, pl.ds(j * 256, 256)], weights.at[j % 2, 0], work_sem.at[3 * (j % 2)])

    def out_step(j):
        at = slice(j * 256, (j + 1) * 256)
        out_in(j).wait()
        if j + 1 < blocks:
            out_in(j + 1).start()
        hidden[:, at] = tokens[:, at].astype(jnp.float32) + dot_nn(gated[...], weights[j % 2, 0])

    hidden_copy = pltpu.make_async_copy(hidden, hidden_out, work_sem.at[12])

    def norm_two_step():
        hidden_copy.start()

        @pl.loop(0, tokens.shape[0] // 64)
        def _(r):
            at = pl.ds(pl.multiple_of(r * 64, 64), 64)
            rows_two = hidden[at, :]
            scale = lax.rsqrt(jnp.mean(rows_two * rows_two, -1, keepdims=True) + EPS)
            normed_two[at, :] = (rows_two * scale * vectors[gain_two : gain_two + 1, :]).astype(jnp.bfloat16)

    shard = depth // 8

    def turned_out():
        copies = []
        for chip in range(4):
            for goal, core_of, sem in ((mine_t, c, 0), (mate_t, 1 - c, 4)):
                start = pl.multiple_of((2 * chip + core_of) * shard, 16)
                copies.append(pltpu.make_async_copy(turned.at[pl.ds(start, shard)], goal.at[pl.ds(chip * shard, shard)], work_sem.at[sem + chip]))
        return copies

    def turn_step():
        @pl.loop(0, blocks)
        def _(r):
            at = pl.ds(pl.multiple_of(r * 256, 256), 256)
            turned[at, :] = normed_two[:, at].T

        start_all(turned_out())

    def each(step, *js):
        return [functools.partial(step, j) for j in js]

    work = {3: [small_step], 5: [norm_one_step]}
    first = 3 * 2 + 5
    work[first] = each(project_step, 0, 1)
    work[first + 1] = each(project_step, 2, 3)
    work[first + 2] = each(project_step, 4, 5) + [edge_start]
    work[first + 3] = [edge_wait] + each(conv_step, *range(blocks))
    work[first + 4] = each(out_step, *range(blocks))
    work[first + 5] = [norm_two_step, turn_step]

    def small_copy(k):
        return remote(small, smalls.at[k - 1], small_send.at[k - 1], small_recv.at[k - 1], (s, lax.rem(f + k, 8)))

    begin(0)
    for k in range(1, 8):
        small_copy(k).start()
    stages = (spread, diagonal, share, finish)
    lag = (0, 1, 3, 5)
    for step in range(3 * count + lag[-1]):
        for stage, by in zip(stages, lag):
            if 0 <= step - by < 3 * count:
                m, j = divmod(step - by, 3)
                stage(m, j)
                if stage is spread and j == 1 and m + 1 < count:
                    begin(m + 1)
        for piece in work.get(step, []):
            piece()
    hidden_copy.wait()
    wait_all(turned_out())


def front(shards, small, tokens, cid):
    count = len(shards)
    anyspec = pl.BlockSpec(memory_space=pl.ANY)
    whole = pl.BlockSpec(memory_space=pltpu.VMEM)
    vmem = pltpu.VMEM
    dma = pltpu.SemaphoreType.DMA
    sds = jax.ShapeDtypeStruct
    rows, depth = tokens.shape
    half, full = jnp.bfloat16, jnp.float32
    outs = [sds((8 * a.shape[0], a.shape[1]), a.dtype) for a in shards]
    outs += [sds((rows, depth), half), sds((rows, 3 * depth), half), sds((2, 8, depth), full), sds((8, depth), full), sds((rows, depth), full)]
    outs += [sds((rows, depth), half), sds((depth // 2, rows), half), sds((depth // 2, rows), half)]
    return pl.pallas_call(
        functools.partial(front_kernel, count),
        out_shape=outs,
        in_specs=[anyspec] * count + [whole] * 2,
        out_specs=[anyspec] * count + [whole, anyspec, whole, whole, anyspec, whole, anyspec, anyspec],
        scratch_shapes=[dma((count,)), dma((count, 4)), dma((count, 4)), dma((count, 5)), dma((count, 3))]
        + [dma((count, 3, 2))] * 4
        + [dma((7,)), dma((7,))]
        + [vmem(a.shape, a.dtype) for a in shards]
        + [vmem((7,) + small.shape, full), vmem((2, 3, depth, 256), half), vmem((2, 3, rows, 256), half), vmem((2, rows // 2 + 8, depth), full)]
        + [vmem((rows, depth), half), vmem((rows, depth), full), vmem((depth, rows), half), dma((13,)), dma, dma],
        compiler_params=pltpu.CompilerParams(collective_id=cid, has_side_effects=True, vmem_limit_bytes=58 << 20),
        name="front",
    )(*shards, small, tokens)


def mix_kernel(plan, kinds, *refs):
    arrays, n = max(p[1] for p in plan) + 1, len(kinds)
    grads = list(refs[: arrays - 2])
    normed, down_in, tokens, edges, taps, gain_one, gain_two, w_in, w_out, projected, back, hidden = refs[arrays - 2 : arrays + 10]
    at = arrays + 10
    outs, small_out, tokens_grad, grad_out, grad_in = refs[at : at + arrays], *refs[at + arrays : at + arrays + 4]
    at += arrays + 4
    grads += [grad_out, grad_in]
    landing = [refs[at + 6 * k : at + 6 * k + 6] for k in range(n)]
    at += 6 * n
    scratch = [refs[at + 6 * k : at + 6 * k + 6] for k in range(n)]
    at += 6 * n
    sems = [refs[at + 13 * k : at + 13 * k + 13] for k in range(n)]
    at += 13 * n
    own_sem, small_own, small_land, small_s, small_r, normed_t, block, weights, normed_grad, residual, work_sem = refs[at : at + 11]
    proj_back, out_back, conv_grad, part, mixed, rows_out, edge_s, edge_r = refs[at + 11 :]
    here = Here()
    here.greet(True)

    def columns(k, t):
        return [p for p in plan if p[0] == k][t]

    reducers = []
    for k, (rows, width) in enumerate(kinds):
        spans = halves(rows)

        def source(t, core, k=k, width=width):
            _, array, column = columns(k, t)
            if array >= arrays - 2:
                whole = grads[array].shape
                return grads[array].reshape(2, 2, 2, 2, 2, whole[0] // 32, whole[1]).at[:, :, core, :, :, :, pl.ds(column, width)]
            return grads[array].at[:, :, core, :, :, :, pl.ds(column, width)]

        def goal(t, quarter, part, k=k, width=width, spans=spans):
            _, array, column = columns(k, t)
            return outs[array].at[quarter, spans[part], pl.ds(column, width)]

        held, total, *fresh = scratch[k]
        red = Reducer(here, False, held, total, fresh, landing[k], sems[k], lambda t, source=source: source(t, 1 - here.c), goal)
        red.own = lambda t, k=k, source=source, red=red: pltpu.make_async_copy(source(t, here.c), red.mine(t), own_sem.at[k])
        reducers.append(red)

    def stage1(red, t):
        red.own(t).start()
        red.fetch1(t)
        red.own(t).wait()
        red.stage1(t)

    def both(name):
        def run(red, t):
            getattr(red, "fetch" + name)(t)
            getattr(red, "stage" + name)(t)

        return run

    hops = [here.mate, (here.beside[0], here.f), (here.beside[1], here.f)]

    def small_hop(j):
        return remote(small_own.at[j], small_land.at[j], small_s.at[j], small_r.at[j], hops[j])

    def small_chip(j):
        a = lax.rem(here.z + j, 4)
        return remote(small_own.at[3], small_land.at[2 + j], small_s.at[2 + j], small_r.at[2 + j], (here.s, 2 * a + here.c))

    def small_step(j):
        if j < 3:
            small_hop(j).wait()
            small_own[j + 1] = small_own[j] + small_land[j]
            if j < 2:
                small_hop(j + 1).start()
            else:
                for i in (1, 2, 3):
                    small_chip(i).start()
        else:
            for i in (1, 2, 3):
                small_chip(i).wait()
            small_out[...] = small_own[3] + small_land[3] + small_land[4] + small_land[5]

    width, depth = proj_back.shape[1], normed.shape[1]
    chunk = block.shape[1]

    def block_out(j):
        return pltpu.make_async_copy(block, grad_in.at[:, pl.ds(j * chunk, chunk)], work_sem.at[0])

    def turn():
        @pl.loop(0, depth // 256)
        def _(r):
            at = pl.ds(pl.multiple_of(r * 256, 256), 256)
            normed_t[at, :] = normed[:, at].T

    def grad_in_step(j):
        if j == 0:
            turn()
        else:
            block_out(j - 1).wait()

        @pl.loop(0, depth // 256)
        def _(r):
            at = pl.ds(pl.multiple_of(r * 256, 256), 256)
            block[at, :] = dot_nn(normed_t[at, :], proj_back[:, j * chunk : (j + 1) * chunk]).astype(jnp.bfloat16)

        block_out(j).start()

    blocks = depth // 256

    def weight_in(j):
        return pltpu.make_async_copy(w_in.at[pl.ds(j * 256, 256)], weights.at[j % 2], work_sem.at[1 + j % 2])

    hidden_in = pltpu.make_async_copy(hidden, residual, work_sem.at[3])
    back_in = pltpu.make_async_copy(back, normed_grad, work_sem.at[4])
    result_out = pltpu.make_async_copy(normed_grad, tokens_grad, work_sem.at[3])

    def back_step(j):
        weight_in(j).wait()
        if j + 1 < blocks:
            weight_in(j + 1).start()
        normed_grad[:, j * 256 : (j + 1) * 256] = dot_nt(proj_back[...], weights[j % 2])

    def norm_step():
        @pl.loop(0, normed.shape[0] // 64)
        def _(r):
            at = pl.ds(pl.multiple_of(r * 64, 64), 64)
            token_rows = tokens[at, :].astype(jnp.float32)
            scale = lax.rsqrt(jnp.mean(token_rows * token_rows, -1, keepdims=True) + EPS)
            unit = token_rows * scale
            grad = normed_grad[at, :]
            small_own[0, 0:1, :] += jnp.sum(grad * unit, 0, keepdims=True)
            inner = grad * gain_one[...]
            normed_grad[at, :] = residual[at, :] + scale * (inner - unit * jnp.mean(inner * unit, -1, keepdims=True))

        result_out.start()
        small_hop(0).start()

    def norm_two_step():
        hidden_in.wait()
        back_in.wait()
        small_own[0] = jnp.zeros(small_own.shape[1:], jnp.float32)

        @pl.loop(0, normed.shape[0] // 64)
        def _(r):
            at = pl.ds(pl.multiple_of(r * 64, 64), 64)
            rows_two = residual[at, :]
            scale = lax.rsqrt(jnp.mean(rows_two * rows_two, -1, keepdims=True) + EPS)
            unit = rows_two * scale
            grad = normed_grad[at, :]
            small_own[0, 4:5, :] += jnp.sum(grad * unit, 0, keepdims=True)
            inner = grad * gain_two[...]
            total = down_in[at, :].astype(jnp.float32) + scale * (inner - unit * jnp.mean(inner * unit, -1, keepdims=True))
            residual[at, :] = total
            out_back[at, :] = total.astype(jnp.bfloat16)

    seqs, length = mixed.shape[0], mixed.shape[1] - 8

    def part_in(j):
        slot = j % 2
        return [
            pltpu.make_async_copy(projected.at[:, pl.ds(g * depth + (j % blocks) * 256, 256)], part.at[slot, g], work_sem.at[5 + 3 * slot + g])
            for g in range(3)
        ]

    def out_weight_in(j):
        return pltpu.make_async_copy(w_out.at[pl.ds(j * 256, 256)], weights.at[j % 2, :, 0:depth], work_sem.at[11 + j % 2])

    def rows_out_copy(j):
        return pltpu.make_async_copy(rows_out, grad_out.at[pl.ds(j * 256, 256)], work_sem.at[0])

    def start_block(j):
        if j < 2 * blocks:
            for copy in part_in(j):
                copy.start()
        if j < blocks:
            out_weight_in(j).start()

    def conv_step(j):
        for copy in part_in(j):
            copy.wait()
        out_weight_in(j).wait()
        start_block(j + 1)
        slot, at = j % 2, slice(j * 256, (j + 1) * 256)
        gated_grad = dot_nt(out_back[...], weights[slot, :, 0:depth])
        if j:
            rows_out_copy(j - 1).wait()
        for q in range(seqs):
            span = slice(q * length, (q + 1) * length)
            out_gate = part[slot, 1, span, :].astype(jnp.float32)
            mixed[q, 0:8, :] = edges[q, :, at]
            mixed[q, 8:, :] = part[slot, 0, span, :].astype(jnp.float32) * part[slot, 2, span, :].astype(jnp.float32)
            shifted = [mixed[q, 6 + k : 6 + k + length, :] for k in range(3)]
            conv = sum(taps[k : k + 1, at] * shifted[k] for k in range(3))
            grad = gated_grad[span, :]
            proj_back[span, depth + j * 256 : depth + (j + 1) * 256] = (grad * conv).astype(jnp.bfloat16)
            part[slot, 1, span, :] = (out_gate * conv).astype(jnp.bfloat16)
            grad = grad * out_gate
            conv_grad[q, 0:length, at] = grad
            for k in range(3):
                small_own[0, 1 + k : 2 + k, at] += jnp.sum(grad * shifted[k], 0, keepdims=True)
        rows_out[...] = dot_tn(part[slot, 1], out_back[...]).astype(jnp.bfloat16)
        rows_out_copy(j).start()

    last = here.s == 3

    def edge_step():
        rows_out_copy(blocks - 1).wait()

        @pl.when(last)
        def _():
            conv_grad[:, length : length + 8, :] = jnp.zeros((seqs, 8, depth), jnp.float32)

        @pl.when(here.s > 0)
        def _():
            remote(conv_grad.at[:, 0:8], conv_grad.at[:, length : length + 8], edge_s, edge_r, (jnp.maximum(here.s - 1, 0), here.f)).start()

    def edge_wait():
        copy = remote(conv_grad.at[:, 0:8], conv_grad.at[:, length : length + 8], edge_s, edge_r, (jnp.maximum(here.s - 1, 0), here.f))

        @pl.when(here.s > 0)
        def _():
            copy.wait_send()

        @pl.when(jnp.logical_not(last))
        def _():
            copy.wait_recv()

    def gate_step(j):
        for copy in part_in(j + blocks):
            copy.wait()
        start_block(j + blocks + 1)
        slot, at = j % 2, slice(j * 256, (j + 1) * 256)
        for q in range(seqs):
            span = slice(q * length, (q + 1) * length)
            grad = sum(taps[2 - k : 3 - k, at] * conv_grad[q, k : k + length, at] for k in range(3))
            proj_back[span, at] = (grad * part[slot, 2, span, :].astype(jnp.float32)).astype(jnp.bfloat16)
            proj_back[span, 2 * depth + j * 256 : 2 * depth + (j + 1) * 256] = (grad * part[slot, 0, span, :].astype(jnp.float32)).astype(jnp.bfloat16)

    def several(*steps):
        def run():
            for step in steps:
                step()

        return run

    columns_done = width // chunk
    start_weights = lambda: weight_in(0).start()
    work = [norm_two_step]
    work += [several(*[functools.partial(conv_step, j) for j in (i, i + 1)]) for i in range(0, blocks, 2)]
    work[-1] = several(work[-1], edge_step)
    work += [several(edge_wait, *[functools.partial(gate_step, j) for j in range(blocks // 2)])]
    work += [several(*[functools.partial(gate_step, j) for j in range(blocks // 2, blocks)], start_weights)]
    work += [functools.partial(grad_in_step, j) for j in range(columns_done)]
    work += [several(lambda: block_out(columns_done - 1).wait(), functools.partial(back_step, 0))]
    work += [functools.partial(back_step, j) for j in range(1, blocks)] + [norm_step]
    work += [functools.partial(small_step, j) for j in range(4)]
    hidden_in.start()
    back_in.start()
    start_block(0)
    stages = (lambda red, t: red.stage0(t), stage1, both("2"), both("3"), both("4"), lambda red, t: red.stage5(t), lambda red, t: red.stage6(t))
    seen = [sum(p[0] == q[0] for p in plan[:i]) for i, q in enumerate(plan)]
    steps = len(plan) + len(stages) - 1
    for step in range(steps):
        for by, stage in enumerate(stages):
            if 0 <= step - by < len(plan):
                stage(reducers[plan[step - by][0]], seen[step - by])
        if step < len(work):
            work[step]()
    result_out.wait()
    for i, p in enumerate(plan):
        reducers[p[0]].to_core(seen[i]).wait_send()


def mix(grads, normed, down_in, tokens, edges, taps, gain_one, gain_two, w_in, w_out, projected, back, hidden, plan, kinds, cid):
    view = lambda g: (2, 2, 2, 2, 2, g.shape[0] // 32, g.shape[1])
    counts = [sum(p[0] == k for p in plan) for k in range(len(kinds))]
    sds = jax.ShapeDtypeStruct
    rows, depth = normed.shape
    seqs = edges.shape[0]
    outs = [sds((4,) + view(g)[5:], jnp.bfloat16) for g in [*grads, w_out, w_in]]
    outs += [sds((8, depth), jnp.float32), sds((rows, depth), jnp.float32), sds(w_out.shape, jnp.bfloat16), sds(w_in.shape, jnp.bfloat16)]
    land, scratch, sems = [], [], []
    for (height, width), count in zip(kinds, counts):
        land += landing_shapes(count, False, height, width)
        scratch += scratch_shapes(4, False, height, width)
        sems += sem_shapes(count)
    whole = pl.BlockSpec(memory_space=pltpu.VMEM)
    vmem = pltpu.VMEM
    res = pl.pallas_call(
        functools.partial(mix_kernel, plan, kinds),
        out_shape=outs + land,
        in_specs=[ANY] * len(grads) + [whole] * 7 + [ANY] * 5,
        out_specs=[ANY] * (len(grads) + 2) + [whole] + [ANY] * (3 + len(land)),
        scratch_shapes=scratch
        + sems
        + [DMA((len(kinds),)), vmem((4, 8, depth), jnp.float32), vmem((6, 8, depth), jnp.float32), DMA((6,)), DMA((6,))]
        + [vmem((depth, rows), jnp.bfloat16), vmem((depth, 768), jnp.bfloat16), vmem((2, 256, w_in.shape[1]), jnp.bfloat16)]
        + [vmem((rows, depth), jnp.float32)] * 2
        + [DMA((13,)), vmem((rows, 3 * depth), jnp.bfloat16), vmem((rows, depth), jnp.bfloat16), vmem((seqs, rows // seqs + 8, depth), jnp.float32)]
        + [vmem((2, 3, rows, 256), jnp.bfloat16), vmem((seqs, rows // seqs + 8, 256), jnp.float32), vmem((256, depth), jnp.bfloat16)]
        + [DMA, DMA],
        compiler_params=pltpu.CompilerParams(collective_id=cid, has_side_effects=True, vmem_limit_bytes=61 << 20),
        name="mix",
    )(*[g.reshape(view(g)) for g in grads], normed, down_in, tokens, edges, taps, gain_one, gain_two, w_in, w_out, projected, back, hidden)
    return res[: len(grads) + 4]


def from_behind(shard, axis, by):
    count = lax.axis_size(axis)
    pairs = [(i, i + by) for i in range(count) if 0 <= i + by < count]
    return lax.ppermute(shard, axis, pairs)


def norm_rows(token_rows, gain):
    scale = lax.rsqrt(jnp.mean(token_rows * token_rows, -1, keepdims=True) + EPS)
    unit = token_rows * scale
    return (scale, unit, (unit * gain).astype(jnp.bfloat16))


def norm_back(grad, scale, unit, gain):
    gain_grad = jnp.sum(grad * unit, 0)
    inner = grad * gain
    return (gain_grad, scale * (inner - unit * jnp.mean(inner * unit, -1, keepdims=True)))


def left_cross(left, right):
    return lax.dot_general(left, right, (((0,), (0,)), ((), ())), preferred_element_type=jnp.float32)


def against(left, weight):
    return lax.dot_general(left, weight, (((1,), (1,)), ((), ())), preferred_element_type=jnp.float32)


def product(left, right):
    return jnp.dot(left, right, preferred_element_type=jnp.float32)


def routed():
    return lax.axis_size("seq") == 4 and lax.axis_size("fsdp") == 8


def gather_all(shards, axis=0):
    return [lax.all_gather(a, "fsdp", axis=axis, tiled=True) for a in shards]


def reduce_all(grads):
    outs = []
    for g in grads:
        part = lax.psum_scatter(g.astype(jnp.bfloat16), "fsdp", scatter_dimension=0, tiled=True)
        outs.append(lax.psum(part, "seq").astype(jnp.float32))
    return outs


def plan_of(grads):
    kinds = [(48, 768), (216, 128)]
    plan = []
    for i, g in enumerate(grads):
        kind = 0 if g.shape[0] == 1536 else 1
        plan += [(kind, i, column) for column in range(0, g.shape[1], kinds[kind][1])]
    return plan, kinds


def plain(tokens, keep_mask, upstream, down_in, gain_one, conv_taps, gain_two, w_in, w_out, w_gate, w_up, w_down):
    count, block_rows, model_width = tokens.shape
    rows = count * block_rows

    def shifted(value, edge, side):
        value = value.reshape(count, block_rows, model_width)
        return jnp.concatenate([edge, value] if side < 0 else [value, edge], 1)

    def window(value, start):
        return value[:, start : start + block_rows].reshape(rows, model_width)

    token_rows = tokens.reshape(rows, model_width).astype(jnp.float32)
    scale_one, unit_one, normed_one = norm_rows(token_rows, gain_one)
    projected = product(normed_one, w_in)
    in_gate = projected[:, :model_width]
    out_gate = projected[:, model_width : 2 * model_width]
    values = projected[:, 2 * model_width :]
    mixed = in_gate * values
    edge_rows = from_behind(mixed.reshape(count, block_rows, model_width)[:, block_rows - 2 :], "seq", 1)
    extended = shifted(mixed, edge_rows, -1)
    conv_out = conv_taps[0] * window(extended, 0) + conv_taps[1] * window(extended, 1) + conv_taps[2] * window(extended, 2)
    gated = (out_gate * conv_out).astype(jnp.bfloat16)
    hidden_one = token_rows + product(gated, w_out)
    scale_two, unit_two, normed_two = norm_rows(hidden_one, gain_two)
    gate_pre = product(normed_two, w_gate)
    up_pre = product(normed_two, w_up)
    sigmoid_gate = jax.nn.sigmoid(gate_pre)
    silu_value = gate_pre * sigmoid_gate
    activated = (silu_value * up_pre).astype(jnp.bfloat16)
    hidden_two = hidden_one + product(activated, w_down)
    output = (keep_mask * hidden_two).astype(jnp.bfloat16)
    grad_down = left_cross(activated, down_in)
    grad_act = against(down_in, w_down)
    gate_back = (grad_act * up_pre * sigmoid_gate * (1.0 + gate_pre * (1.0 - sigmoid_gate))).astype(jnp.bfloat16)
    up_back = (grad_act * silu_value).astype(jnp.bfloat16)
    grad_gate = left_cross(normed_two, gate_back)
    grad_up = left_cross(normed_two, up_back)
    grad_normed_two = against(gate_back, w_gate) + against(up_back, w_up)
    grad_gain_two, through_two = norm_back(grad_normed_two, scale_two, unit_two, gain_two)
    grad_hidden = upstream + through_two
    out_back = grad_hidden.astype(jnp.bfloat16)
    grad_out = left_cross(gated, out_back)
    grad_gated = against(out_back, w_out)
    grad_out_gate = grad_gated * conv_out
    grad_conv = grad_gated * out_gate
    edge_grad = from_behind(grad_conv.reshape(count, block_rows, model_width)[:, :2], "seq", -1)
    grad_ext = shifted(grad_conv, edge_grad, 1)
    grad_mixed = conv_taps[2] * window(grad_ext, 0) + conv_taps[1] * window(grad_ext, 1) + conv_taps[0] * window(grad_ext, 2)
    grad_taps = [jnp.sum(grad_conv * window(extended, offset), 0) for offset in range(3)]
    proj_back = jnp.concatenate([grad_mixed * values, grad_out_gate, grad_mixed * in_gate], 1).astype(jnp.bfloat16)
    grad_in = left_cross(normed_one, proj_back)
    grad_normed_one = against(proj_back, w_in)
    grad_gain_one, through_one = norm_back(grad_normed_one, scale_one, unit_one, gain_one)
    tokens_grad = grad_hidden + through_one
    small_grads = jnp.stack([grad_gain_one, *grad_taps, grad_gain_two])
    return output, tokens_grad, small_grads, grad_in, grad_out, grad_gate, grad_up, grad_down


def local(tokens, lengths, norm_gain, in_weight, conv_weight, out_weight, ffn_gain, gate_weight, up_weight, down_weight, cotangent):
    count, block_rows, model_width = tokens.shape
    rows = count * block_rows
    width = norm_gain.shape[0]
    rank = lax.axis_index("fsdp")
    small = jnp.concatenate([norm_gain[None], conv_weight, ffn_gain[None]], 0).astype(jnp.float32)
    window = lambda size, start: lax.dynamic_update_slice(jnp.zeros((8, size), jnp.float32), small, (0, start))
    places = lax.axis_index("seq") * block_rows + jnp.arange(block_rows, dtype=jnp.int32)
    keep_mask = (places[None, :] < lengths[:, None]).astype(jnp.float32).reshape(rows, 1)
    upstream = cotangent.reshape(rows, model_width).astype(jnp.float32) * keep_mask
    down_in = upstream.astype(jnp.bfloat16)
    if routed():
        shards = [out_weight, in_weight, gate_weight, up_weight, down_weight]
        token_rows = tokens.reshape(rows, model_width)
        w_out, w_in, w_gate, w_up, w_down, normed_one, projected, edges, vectors, hidden_one, normed_two, mine_t, mate_t = front(shards, window(256, rank * width % 128), token_rows, 0)
        output, grad_normed_two, grad_down, ffn_sums = ffn(normed_two, mine_t, mate_t, down_in, keep_mask, w_gate, w_up, w_down, hidden_one, 1)
        grad_down, grad_out, grad_in, small_grads, tokens_grad = mix(
            [grad_down], normed_one, down_in, token_rows, edges, vectors[1:4], vectors[0:1], vectors[4:5],
            w_in, w_out, projected, grad_normed_two, hidden_one, *plan_of([grad_down, w_out, w_in]), 2,
        )[:5]
        shards = [grad_down, grad_out, grad_in, ffn_sums[0], ffn_sums[1]]
        grad_down, grad_out, grad_in, grad_gate, grad_up = [g.reshape(-1, g.shape[-1]).astype(jnp.float32) for g in shards]
    else:
        w_in, w_out, w_gate, w_up, w_down = gather_all([in_weight, out_weight, gate_weight, up_weight, down_weight])
        vectors = lax.psum(window(model_width, rank * width), "fsdp")
        output, tokens_grad, small_grads, *grads = plain(
            tokens, keep_mask, upstream, down_in, vectors[0], vectors[1:4], vectors[4], w_in, w_out, w_gate, w_up, w_down
        )
        grad_in, grad_out, grad_gate, grad_up, grad_down = reduce_all(grads)
        small_grads = lax.psum(small_grads, ("seq", "fsdp"))
    small_grads = lax.dynamic_slice_in_dim(small_grads, lax.axis_index("fsdp") * width, width, 1)
    return (
        output.reshape(tokens.shape),
        tokens_grad.reshape(tokens.shape),
        small_grads[0],
        grad_in,
        small_grads[1:4],
        grad_out,
        small_grads[4],
        grad_gate,
        grad_up,
        grad_down,
    )


def solution(mesh):
    split = P("fsdp", "seq", None)
    rows, columns, vector = P("fsdp", None), P(None, "fsdp"), P("fsdp")
    return jax.shard_map(
        local,
        mesh=mesh,
        in_specs=(split, vector, vector, rows, columns, rows, vector, rows, rows, rows, split),
        out_specs=(split, split, vector, rows, columns, rows, vector, rows, rows, rows),
        check_vma=False,
    )
```

profile of v0, /device:TPU:0, one launch (start us, length us, event | category | flops | bytes accessed | tf_op | source)
XLA Modules:
  0.0 845.2 jit_solution(11211282483707350501)
XLA Ops:
  0.7 0.7 broadcast_in_dim.12
  1.3 0.7 broadcast_in_dim.13
  2.0 0.7 fusion.1
  2.7 0.7 maximum_convert_fusion
  3.4 0.4 dynamic_update_slice.3.refs_5_
  3.8 0.0 copy-start.3
  3.9 0.9 copy.23
  4.8 3.5 fusion.down_in.refs_2_
  8.3 0.0 copy-done.3
  8.3 288.3 %front.1 = (bf16[1536,1536]{1,0:T(8,128)(2,1)}, bf16[1536,4608]{1,0:T(8,128)(2,1)}, bf16[1536,6912]{1,0:T(8,128)(2,1)}, bf16[1536,6912]{1,0:T(8,128)(2,1)}, bf16...) custom-call(bf16[192,1536]{1,0:T(8,128)(2,1)} %refs_0_.1, ...), custom_call_target="tpu_custom_call" | custom-call | tf_op jit(solution)/shard_map/front/pallas_call | solution.py:712
  296.6 1.5 fusion.4
  298.1 1.4 slice.24.refs_5_
  299.5 273.9 %ffn.1 = (bf16[768,1536]{1,0:T(8,128)(2,1)}, f32[768,1536]{1,0:T(8,128)}, bf16[6912,1536]{1,0:T(8,128)(2,1)}, bf16[2,4,48,6912]{3,2,1,0:T(8,128)(2,1)}, bf16[9,2...) custom-call(bf16[768,1536]{1,0:T(8,128)(2,1)} %get-tuple-element.32., ...), custom_call_target="tpu_custom_call" | custom-call | tf_op jit(solution)/shard_map/ffn/pallas_call | solution.py:360
  573.4 2.9 fusion.2
  576.3 5.2 bitcast_convert_fusion.1
  581.5 248.8 %mix.1 = (bf16[4,216,1536]{2,1,0:T(8,128)(2,1)}, bf16[4,48,1536]{2,1,0:T(8,128)(2,1)}, bf16[4,48,4608]{2,1,0:T(8,128)(2,1)}, f32[8,1536]{1,0:T(8,128)}, f32[768,...) custom-call(bf16[2,2,2,2,2,216,1536]{6,5,4,3,2,1,0:T(8,128)(2,1)} %b, ...), custom_call_target="tpu_custom_call" | custom-call | tf_op jit(solution)/shard_map/mix/pallas_call | solution.py:1012
  830.4 0.0 copy-start.2
  830.4 1.5 fusion.3
  831.9 1.4 dynamic-slice.1
  833.2 0.0 copy-start
  833.2 2.4 bitcast_convert_fusion.4
  835.6 0.0 copy-done.2
  835.6 0.0 slice-start
  835.6 2.3 bitcast_convert_fusion.3
  837.9 0.0 copy-done
  837.9 0.0 copy-start.1
  837.9 0.0 slice-start.1
  837.9 3.3 bitcast_convert_fusion
  841.2 0.0 copy-done.1
  841.2 1.4 copy.27
  842.6 0.0 slice-done
  842.6 0.0 slice-done.1
  842.6 2.2 copy.28
  (5 shorter events, 0.0 us)
Async XLA Ops:
  3.8 4.5 copy-start.3
  830.4 5.2 copy-start.2
  833.2 4.7 copy-start
  835.6 7.0 slice-start
  837.9 3.3 copy-start.1
  837.9 4.7 slice-start.1
where the time goes:
time: 857 us; the launch traced here: 845 us
  Pallas kernels  811 us (95%)
  other arithmetic  18 us (2%)
  local copies, waits for them, and re-layouts  15 us (2%)
    pallas_call x1, Pallas kernels, front(): pl.pallas_call(functools.partial(front_kernel, count), out_shape=outs, in...  288 us
    pallas_call x1, Pallas kernels, ffn(): pl.pallas_call(functools.partial(ffn_kernel, tiles), grid=(tiles + 17,),...  274 us
    pallas_call x1, Pallas kernels, mix(): pl.pallas_call(functools.partial(mix_kernel, plan, kinds), out_shape=outs...  249 us

commit v1 on v0

--- a/solution.py
+++ b/solution.py
@@ -740,7 +740,7 @@
     sems = [refs[at + 13 * k : at + 13 * k + 13] for k in range(n)]
     at += 13 * n
     own_sem, small_own, small_land, small_s, small_r, normed_t, block, weights, normed_grad, residual, work_sem = refs[at : at + 11]
-    proj_back, out_back, conv_grad, part, mixed, rows_out, edge_s, edge_r = refs[at + 11 :]
+    proj_back, out_back, conv_grad, part, mixed, edge_s, edge_r = refs[at + 11 :]
     here = Here()
     here.greet(True)
 
@@ -767,18 +767,13 @@
         red.own = lambda t, k=k, source=source, red=red: pltpu.make_async_copy(source(t, here.c), red.mine(t), own_sem.at[k])
         reducers.append(red)
 
-    def stage1(red, t):
+    def ahead(red, t):
         red.own(t).start()
         red.fetch1(t)
+
+    def stage1(red, t):
         red.own(t).wait()
         red.stage1(t)
-
-    def both(name):
-        def run(red, t):
-            getattr(red, "fetch" + name)(t)
-            getattr(red, "stage" + name)(t)
-
-        return run
 
     hops = [here.mate, (here.beside[0], here.f), (here.beside[1], here.f)]
 
@@ -888,8 +883,11 @@
     def out_weight_in(j):
         return pltpu.make_async_copy(w_out.at[pl.ds(j * 256, 256)], weights.at[j % 2, :, 0:depth], work_sem.at[11 + j % 2])
 
-    def rows_out_copy(j):
-        return pltpu.make_async_copy(rows_out, grad_out.at[pl.ds(j * 256, 256)], work_sem.at[0])
+    def rows_out(j):
+        return [
+            pltpu.make_async_copy(block.at[pl.ds(h * 256, 256)], grad_out.at[pl.ds(j * 256, 256), pl.ds(h * chunk, chunk)], work_sem.at[13 * h])
+            for h in (0, 1)
+        ]
 
     def start_block(j):
         if j < 2 * blocks:
@@ -906,7 +904,8 @@
         slot, at = j % 2, slice(j * 256, (j + 1) * 256)
         gated_grad = dot_nt(out_back[...], weights[slot, :, 0:depth])
         if j:
-            rows_out_copy(j - 1).wait()
+            for copy in rows_out(j - 1):
+                copy.wait()
         for q in range(seqs):
             span = slice(q * length, (q + 1) * length)
             out_gate = part[slot, 1, span, :].astype(jnp.float32)
@@ -921,13 +920,15 @@
             conv_grad[q, 0:length, at] = grad
             for k in range(3):
                 small_own[0, 1 + k : 2 + k, at] += jnp.sum(grad * shifted[k], 0, keepdims=True)
-        rows_out[...] = dot_tn(part[slot, 1], out_back[...]).astype(jnp.bfloat16)
-        rows_out_copy(j).start()
+        for h, copy in enumerate(rows_out(j)):
+            block[h * 256 : (h + 1) * 256, :] = dot_tn(part[slot, 1], out_back[:, h * chunk : (h + 1) * chunk]).astype(jnp.bfloat16)
+            copy.start()
 
     last = here.s == 3
 
     def edge_step():
-        rows_out_copy(blocks - 1).wait()
+        for copy in rows_out(blocks - 1):
+            copy.wait()
 
         @pl.when(last)
         def _():
@@ -974,21 +975,27 @@
     work += [several(edge_wait, *[functools.partial(gate_step, j) for j in range(blocks // 2)])]
     work += [several(*[functools.partial(gate_step, j) for j in range(blocks // 2, blocks)], start_weights)]
     work += [functools.partial(grad_in_step, j) for j in range(columns_done)]
-    work += [several(lambda: block_out(columns_done - 1).wait(), functools.partial(back_step, 0))]
-    work += [functools.partial(back_step, j) for j in range(1, blocks)] + [norm_step]
+    work += [several(lambda: block_out(columns_done - 1).wait(), functools.partial(back_step, 0), functools.partial(back_step, 1))]
+    work += [several(*[functools.partial(back_step, j) for j in (i, i + 1)]) for i in range(2, blocks, 2)] + [norm_step]
     work += [functools.partial(small_step, j) for j in range(4)]
     hidden_in.start()
     back_in.start()
     start_block(0)
-    stages = (lambda red, t: red.stage0(t), stage1, both("2"), both("3"), both("4"), lambda red, t: red.stage5(t), lambda red, t: red.stage6(t))
+    stages = [(0, "stage0"), (1, "stage1"), (2, "fetch2"), (3, "fetch3"), (4, "fetch4"), (2, "stage2"), (3, "stage3"), (4, "stage4"), (5, "stage5"), (6, "stage6")]
     seen = [sum(p[0] == q[0] for p in plan[:i]) for i, q in enumerate(plan)]
-    steps = len(plan) + len(stages) - 1
-    for step in range(steps):
-        for by, stage in enumerate(stages):
+    assert len(work) <= len(plan) + 6
+    for step in range(len(plan) + 6):
+        for by, name in stages:
             if 0 <= step - by < len(plan):
-                stage(reducers[plan[step - by][0]], seen[step - by])
+                red, t = reducers[plan[step - by][0]], seen[step - by]
+                if name == "stage1":
+                    stage1(red, t)
+                else:
+                    getattr(red, name)(t)
         if step < len(work):
             work[step]()
+        if step < len(plan):
+            ahead(reducers[plan[step][0]], seen[step])
     result_out.wait()
     for i, p in enumerate(plan):
         reducers[p[0]].to_core(seen[i]).wait_send()
@@ -1019,10 +1026,10 @@
         + [DMA((len(kinds),)), vmem((4, 8, depth), jnp.float32), vmem((6, 8, depth), jnp.float32), DMA((6,)), DMA((6,))]
         + [vmem((depth, rows), jnp.bfloat16), vmem((depth, 768), jnp.bfloat16), vmem((2, 256, w_in.shape[1]), jnp.bfloat16)]
         + [vmem((rows, depth), jnp.float32)] * 2
-        + [DMA((13,)), vmem((rows, 3 * depth), jnp.bfloat16), vmem((rows, depth), jnp.bfloat16), vmem((seqs, rows // seqs + 8, depth), jnp.float32)]
-        + [vmem((2, 3, rows, 256), jnp.bfloat16), vmem((seqs, rows // seqs + 8, 256), jnp.float32), vmem((256, depth), jnp.bfloat16)]
+        + [DMA((14,)), vmem((rows, 3 * depth), jnp.bfloat16), vmem((rows, depth), jnp.bfloat16), vmem((seqs, rows // seqs + 8, depth), jnp.float32)]
+        + [vmem((2, 3, rows, 256), jnp.bfloat16), vmem((seqs, rows // seqs + 8, 256), jnp.float32)]
         + [DMA, DMA],
-        compiler_params=pltpu.CompilerParams(collective_id=cid, has_side_effects=True, vmem_limit_bytes=61 << 20),
+        compiler_params=pltpu.CompilerParams(collective_id=cid, has_side_effects=True, vmem_limit_bytes=62 << 20),
         name="mix",
     )(*[g.reshape(view(g)) for g in grads], normed, down_in, tokens, edges, taps, gain_one, gain_two, w_in, w_out, projected, back, hidden)
     return res[: len(grads) + 4]
@@ -1075,7 +1082,7 @@
 
 
 def plan_of(grads):
-    kinds = [(48, 768), (216, 128)]
+    kinds = [(48, 768), (216, 256)]
     plan = []
     for i, g in enumerate(grads):
         kind = 0 if g.shape[0] == 1536 else 1

time: 857 us -> 853 us (level)
  no operation moved by 1% of the time
where the time goes in v1:
time: 853 us; the launch traced here: 843 us
  Pallas kernels  809 us (95%)
  other arithmetic  18 us (2%)
  local copies, waits for them, and re-layouts  15 us (2%)
    pallas_call x1, Pallas kernels, front(): pl.pallas_call(functools.partial(front_kernel, count), out_shape=outs, in...  288 us
    pallas_call x1, Pallas kernels, ffn(): pl.pallas_call(functools.partial(ffn_kernel, tiles), grid=(tiles + 17,),...  274 us
    pallas_call x1, Pallas kernels, mix(): pl.pallas_call(functools.partial(mix_kernel, plan, kinds), out_shape=outs...  246 us

profile of v1, /device:TPU:0, one launch (start us, length us, event | category | flops | bytes accessed | tf_op | source)
XLA Modules:
  0.0 842.9 jit_solution(2215301548876677845)
XLA Ops:
  0.7 0.7 broadcast_in_dim.12
  1.3 0.7 broadcast_in_dim.13
  2.0 0.7 fusion.1
  2.7 0.7 maximum_convert_fusion
  3.4 0.4 dynamic_update_slice.3.refs_5_
  3.8 0.0 copy-start.3
  3.9 0.9 copy.23
  4.8 3.5 fusion.down_in.refs_2_
  8.3 0.0 copy-done.3
  8.3 288.3 %front.1 = (bf16[1536,1536]{1,0:T(8,128)(2,1)}, bf16[1536,4608]{1,0:T(8,128)(2,1)}, bf16[1536,6912]{1,0:T(8,128)(2,1)}, bf16[1536,6912]{1,0:T(8,128)(2,1)}, bf16...) custom-call(bf16[192,1536]{1,0:T(8,128)(2,1)} %refs_0_.1, ...), custom_call_target="tpu_custom_call" | custom-call | tf_op jit(solution)/shard_map/front/pallas_call | solution.py:712
  296.6 1.5 fusion.4
  298.1 1.4 slice.24.refs_5_
  299.5 273.9 %ffn.1 = (bf16[768,1536]{1,0:T(8,128)(2,1)}, f32[768,1536]{1,0:T(8,128)}, bf16[6912,1536]{1,0:T(8,128)(2,1)}, bf16[2,4,48,6912]{3,2,1,0:T(8,128)(2,1)}, bf16[9,2...) custom-call(bf16[768,1536]{1,0:T(8,128)(2,1)} %get-tuple-element.32., ...), custom_call_target="tpu_custom_call" | custom-call | tf_op jit(solution)/shard_map/ffn/pallas_call | solution.py:360
  573.4 2.9 fusion.2
  576.3 5.2 bitcast_convert_fusion.1
  581.5 246.5 %mix.1 = (bf16[4,216,1536]{2,1,0:T(8,128)(2,1)}, bf16[4,48,1536]{2,1,0:T(8,128)(2,1)}, bf16[4,48,4608]{2,1,0:T(8,128)(2,1)}, f32[8,1536]{1,0:T(8,128)}, f32[768,...) custom-call(bf16[2,2,2,2,2,216,1536]{6,5,4,3,2,1,0:T(8,128)(2,1)} %b, ...), custom_call_target="tpu_custom_call" | custom-call | tf_op jit(solution)/shard_map/mix/pallas_call | solution.py:1019
  828.0 0.0 copy-start.2
  828.0 1.5 fusion.3
  829.5 1.4 dynamic-slice.1
  830.9 0.0 copy-start
  830.9 2.4 bitcast_convert_fusion.4
  833.2 0.0 copy-done.2
  833.2 0.0 slice-start
  833.2 2.3 bitcast_convert_fusion.3
  835.5 0.0 copy-done
  835.5 0.0 copy-start.1
  835.5 0.0 slice-start.1
  835.5 3.3 bitcast_convert_fusion
  838.8 0.0 copy-done.1
  838.8 1.4 copy.27
  840.2 0.0 slice-done
  840.2 0.0 slice-done.1
  840.2 2.2 copy.28
  (5 shorter events, 0.0 us)
Async XLA Ops:
  3.8 4.5 copy-start.3
  828.0 5.2 copy-start.2
  830.9 4.7 copy-start
  833.2 7.0 slice-start
  835.5 3.3 copy-start.1
  835.5 4.7 slice-start.1
